TPU v7x, 128 devices: a whole 4x4x4 slice. The times are simulated.
128 devices in a mesh: pw: 8 (over x_lo, y), pair: 16 (over z, x_hi, core).
Axes of the slice: x: 4 (x_hi: 2, x_lo: 2; x = x_hi * 2 + x_lo), y: 4, z: 4, core: 2. Of those that a mesh axis runs over, the one named last changes fastest.
Arguments:
- pair_waves: bfloat16 [16384, 16384], P('pair', 'pw'), may hold values from -6 to 6
- subspace_basis: bfloat16 [16384, 1024], P('pw'), may hold values from -0.0625 to 0.0625
- occ_band: int32 [16384], P('pair'), may hold values from 0 to 63, as said below
- empty_band: int32 [16384], P('pair'), may hold values from 0 to 255, as said below
- occ_energy: float32 [64], replicated, may hold values from -3 to -0.25
- empty_energy: float32 [256], replicated, may hold values from 0.25 to 6
- freq_grid: float32 [16], replicated, may hold values from 0.5 to 6
- freq_index: int32 [16], replicated, may hold values from 0 to 15, each once
Outputs:
- chi_tiles: float32 [16, 1024, 1024], P(None, 'pw', 'pair')
Inputs may be any that keep to these rules, and one draw needn't show every extreme that they name: `freq_index`: each frequency slot names a different grid point. `occ_band`: no two pairs have the same occupied band and the same empty band. `empty_band`: no two pairs have the same occupied band and the same empty band.
All inputs are finite; a program needn't handle non-finite values.
Results may differ from a plain program's by a relative error of at most 0.017.
Values may be sent and summed in bfloat16 or wider, within the bound.
A program may use at most 64 MiB of HBM per device.

v0:
```python
import jax
import jax.numpy as jnp
from jax import lax
from jax.sharding import PartitionSpec as P

broadening_sq = 0.0025


def in_blocks(shard, dim, count):
    before, after = (shard.shape[:dim], shard.shape[dim + 1 :])
    return jnp.moveaxis(shard.reshape(*before, count, -1, *after), dim, 0)


def sent_and_summed(shard, axis, dim):
    parts = in_blocks(shard, dim, lax.axis_size(axis))
    arrived = lax.all_to_all(parts, axis, split_axis=0, concat_axis=0, tiled=True)
    return arrived.astype(jnp.float32).sum(axis=0)


def in_order(parts, dim):
    lengths = list(parts.shape[1:])
    lengths[dim] *= parts.shape[0]
    return jnp.moveaxis(parts, 0, dim).reshape(lengths)


def copy_for_each(shard, axis):
    count = lax.axis_size(axis)
    return lax.all_to_all(
        jnp.broadcast_to(shard[None], (count, *shard.shape)), axis, 0, 0, tiled=True
    )


def collect(shard, axis, dim):
    return in_order(copy_for_each(shard, axis), dim)


def lookup(indices, values_table):
    positions = jnp.arange(values_table.shape[0], dtype=jnp.int32)
    hits = indices[:, None] == positions[None, :]
    return jnp.sum(
        jnp.where(hits, values_table[None, :], jnp.zeros_like(values_table)[None, :]), axis=1
    )


def response(frequency, energy_gap):
    below = frequency[:, None] - energy_gap[None, :]
    above = frequency[:, None] + energy_gap[None, :]
    return below / (below * below + broadening_sq) - above / (above * above + broadening_sq)


def on_device(
    pair_waves,
    subspace_basis,
    occ_band,
    empty_band,
    occ_energy,
    empty_energy,
    freq_grid,
    freq_index,
):
    pair_local = pair_waves.shape[0]
    row_block = sent_and_summed(
        lax.dot_general(
            subspace_basis, pair_waves, (((0,), (1,)), ((), ())), preferred_element_type=jnp.float32
        ).astype(jnp.bfloat16),
        "pw",
        0,
    ).astype(jnp.bfloat16)
    projected = collect(row_block, "pw", 0)
    col_all = lax.all_to_all(projected, "pair", split_axis=0, concat_axis=1, tiled=True)
    energy_gap = lookup(empty_band, empty_energy) - lookup(occ_band, occ_energy)
    frequency = lookup(freq_index, freq_grid)
    prefactor = 4.0 / (pair_local * lax.axis_size("pair"))
    factor = prefactor * response(frequency, energy_gap)
    rows_piece = lax.all_gather(row_block, "pair", axis=1, tiled=True)
    factor_piece = lax.all_gather(factor.astype(jnp.bfloat16), "pair", axis=1, tiled=True).astype(
        jnp.float32
    )
    weighted = (rows_piece.astype(jnp.float32)[None, :, :] * factor_piece[:, None, :]).astype(
        jnp.bfloat16
    )
    return jnp.einsum("fsp,tp->fst", weighted, col_all, preferred_element_type=jnp.float32)


def solution(mesh):
    return jax.shard_map(
        on_device,
        mesh=mesh,
        in_specs=(P("pair", "pw"), P("pw", None), P("pair"), P("pair"), P(), P(), P(), P()),
        out_specs=P(None, "pw", "pair"),
        check_vma=False,
    )
```

profile of v0, /device:TPU:1, one launch (start us, length us, event | category | flops | bytes accessed | tf_op | source)
XLA Modules:
  0.0 175.9 jit_solution(18210863068671004381)
XLA Ops:
  6.5 8.0 %convolution_convert_fusion = bf16[1024,1024]{1,0:T(8,128)(2,1)S(1)} fusion(bf16[2048,1024]{1,0:T(8,128)(2,1)} %param.9, bf16[1024,2048]{1,0:T(8,128)(2,1)} %param.8), kind=kOutput, calls=%fused_computation.4 | convolution fusion | flops 4296015872 | bytes 10485760 | tf_op jit(solution)/shard_map/dot_general | solution.py:63
  14.5 31.5 %all_to_all.29 = bf16[8,128,1024]{2,1,0:T(8,128)(2,1)S(1)} all-to-all(bf16[8,128,1024]{2,1,0:T(8,128)(2,1)S(1)} %bitcast.8), channel_id=1, replica_groups=mesh['pw'=8,'pair'=16] {'pw'}, dimensions={0} | all-to-all | bytes 4194304 | tf_op jit(solution)/shard_map/all_to_all | solution.py:16
  46.0 1.1 reduce_sum.39
  47.1 0.0 all-gather.2.cloned.1.call-update
  47.1 1.2 broadcast_in_dim.75
  48.4 0.0 copy-start
  48.4 0.0 copy-start.3
  48.4 0.0 copy-start.1
  48.4 0.0 copy-start.2
  48.4 0.0 copy-start.4
  48.4 0.0 copy-start.5
  48.4 30.2 %all_to_all.30 = bf16[8,128,1024]{2,1,0:T(8,128)(2,1)} all-to-all(bf16[8,128,1024]{2,1,0:T(8,128)(2,1)S(1)} %broadcast_in_dim.75), channel_id=1, replica_groups=mesh['pw'=8,'pair'=16] {'pw'}, dimensions={0} | all-to-all | bytes 4194304 | tf_op jit(solution)/shard_map/all_to_all | solution.py:28
  78.6 11.4 %all-to-all-start.2 = ((bf16[16,64,1024]{2,1,0:T(8,128)(2,1)}), bf16[16,64,1024]{2,1,0:T(8,128)(2,1)S(1)}, u32[]{:S(2)}, u32[]{:S(2)}) async-start(bf16[16,64,1024]{2,1,0:T(8,128)(2,1)} %bitcast.7), calls=%async_computation.2 | async-start | bytes 4194304 | tf_op jit(solution)/shard_map/all_to_all | solution.py:70
  90.0 0.1 select_reduce_fusion.1
  90.1 0.4 select_reduce_fusion
  90.5 0.2 select_reduce_fusion.2
  90.7 0.1 fusion.7
  90.8 48.2 %all_gather.7 = bf16[16,16384]{1,0:T(8,128)(2,1)S(1)} all-gather(bf16[16,1024]{1,0:T(8,128)(2,1)S(1)} %fusion.7), channel_id=1, replica_groups=mesh['pw'=8,'pair'=16] {'pair'}, dimensions={1}, use_global_device_ids=true | all-gather | bytes 557056 | tf_op jit(solution)/shard_map/all_gather | solution.py:76
  139.0 0.1 convert_element_type.20
  139.1 2.5 %copy.10 = bf16[64,16,1024]{2,1,0:T(8,128)(2,1)} copy(bf16[64,16,1024]{2,0,1:T(8,128)(2,1)S(1)} %bitcast.6) | data formatting | bytes 4194304 | tf_op jit(solution)/shard_map/all_to_all | solution.py:70
  141.6 2.9 %reshape.24 = bf16[64,16384,1]{1,0,2:T(8,128)(2,1)S(1)} reshape(bf16[64,16,1024]{2,1,0:T(8,128)(2,1)} %copy.10) | data formatting | bytes 4194304 | tf_op jit(solution)/shard_map/all_to_all | solution.py:70
  144.5 0.0 all-gather.2.cloned.1.call-done
  144.5 3.0 %convert_element_type.18 = f32[128,16384]{1,0:T(8,128)S(1)} convert(bf16[128,16384]{1,0:T(8,128)(2,1)} %all-gather.2.cloned.1.call-done) | non-fusion elementwise | flops 2097152 | bytes 12582912 | tf_op jit(solution)/shard_map/convert_element_type | solution.py:79
  147.6 21.5 %fusion = f32[16,128,64]{1,2,0:T(8,128)} fusion(bf16[64,16384,1]{1,0,2:T(8,128)(2,1)S(1)} %reshape.24, f32[16,16384]{1,0:T(8,128)S(1)} %convert_element_type.20, f32[128,16384]{1,0:T(8,128)S(1)} %convert_element_type.18), kind=kOutput, calls=%fused_computation.1 | convolution fusion | flops 4362076160 | bytes 12058624 | tf_op jit(solution)/shard_map/fsp,tp->fst/dot_general | solution.py:82
  (9 shorter events, 0.0 us)
Async XLA Ops:
  6.5 138.0 %all-gather.2.cloned.1.call-start = ((), (), s32[]{:S(2)}) async-start(), calls=%async_computation.3 | async-start | bytes 4456448 | tf_op jit(solution)/shard_map/all_gather | solution.py:75
  48.4 41.6 %copy-start = (s32[1024]{0:T(1024)S(1)}, s32[1024]{0:T(1024)}, u32[]{:S(2)}) copy-start(s32[1024]{0:T(1024)} %param.10) | copy-start | bytes 12292
  48.4 41.6 %copy-start.3 = (f32[64]{0:T(128)S(1)}, f32[64]{0:T(128)}, u32[]{:S(2)}) copy-start(f32[64]{0:T(128)} %param.12) | copy-start | bytes 772
  48.4 41.7 %copy-start.1 = (s32[1024]{0:T(1024)S(1)}, s32[1024]{0:T(1024)}, u32[]{:S(2)}) copy-start(s32[1024]{0:T(1024)} %param.11) | copy-start | bytes 12292
  48.4 41.7 %copy-start.2 = (f32[256]{0:T(256)S(1)}, f32[256]{0:T(256)}, u32[]{:S(2)}) copy-start(f32[256]{0:T(256)} %param.13) | copy-start | bytes 3076
  48.4 42.1 %copy-start.4 = (f32[16]{0:T(128)S(1)}, f32[16]{0:T(128)}, u32[]{:S(2)}) copy-start(f32[16]{0:T(128)} %param.14) | copy-start | bytes 196
  48.4 42.1 %copy-start.5 = (s32[16]{0:T(128)S(1)}, s32[16]{0:T(128)}, u32[]{:S(2)}) copy-start(s32[16]{0:T(128)} %param.15) | copy-start | bytes 196
  78.6 60.5 %all-to-all-start.2 = ((bf16[16,64,1024]{2,1,0:T(8,128)(2,1)}), bf16[16,64,1024]{2,1,0:T(8,128)(2,1)S(1)}, u32[]{:S(2)}, u32[]{:S(2)}) async-start(bf16[16,64,1024]{2,1,0:T(8,128)(2,1)} %bitcast.7), calls=%async_computation.2 | async-start | bytes 4194304 | tf_op jit(solution)/shard_map/all_to_all | solution.py:70
Sparse Core Ops, SparseCore 0:
  47.3 72.6 all-gather.1
where the time goes:
time: 176 us
  blocking collectives  110 us (62%)
  matrix products  29.5 us (17%)
  between operations  13.6 us (8%)
  starting transfers between devices  11.4 us (6%)
  local copies, waits for them, and re-layouts  6.6 us (4%)
  other arithmetic  4.95 us (3%)
    all_gather x1, blocking collectives, on_device(): lax.all_gather(factor.astype(jnp.bfloat16), 'pair', axis=1, tiled=True)  48.2 us
    all_to_all x1, blocking collectives, sent_and_summed(): lax.all_to_all(parts, axis, split_axis=0, concat_axis=0, tiled=True)  31.5 us
    all_to_all x1, blocking collectives, copy_for_each(): lax.all_to_all(jnp.broadcast_to(shard[None], (count, *shard.shape)), axis...  30.2 us
    dot_general x1, matrix products, on_device(): jnp.einsum('fsp,tp->fst', weighted, col_all, preferred_element_type=jnp.f...  21.5 us
    all_to_all x1, starting transfers between devices, on_device(): lax.all_to_all(projected, 'pair', split_axis=0, concat_axis=1, tiled=True)  11.4 us
    dot_general x1, matrix products, on_device(): lax.dot_general(subspace_basis, pair_waves, (((0,), (1,)), ((), ())), pre...  8 us
    all_to_all x2, local copies, waits for them, and re-layouts, on_device(): lax.all_to_all(projected, 'pair', split_axis=0, concat_axis=1, tiled=True)  5.36 us
  transfers between devices with their start and end apart: 2, of which 0 were waited for; matrix products, arithmetic and copies ran while one was open for 4% of the time, Pallas kernels for 0%

commit v1 on v0

v1 whole, which is shorter than its diff:
```python
import jax
import jax.numpy as jnp
from jax import lax
from jax.experimental import pallas as pl
from jax.experimental.pallas import tpu as pltpu
from jax.sharding import PartitionSpec as P

F32, BF16 = jnp.float32, jnp.bfloat16
MESH = pl.DeviceIdType.MESH
broadening_sq = 0.0025

PAIRS = 16384
NFREQ = 16
NW = 8
NB = 1024
PL = 1024
PWL = 2048
ROWS = 128
NC = 4
CP = PL // NC
BP = CP // 4
HP = BP // 2
NQ = 4
QR = NW * ROWS // NQ
ZC = NB // 4
XC = ZC // 2


def kernel(
    occ_ref, emp_ref, pw_hbm, basis_hbm, oe_ref, ee_ref, fg_ref, fi_ref, out_ref,
    pw, basis, part, cf, acc, wt, gaps, fac,
    ta, tb, sa, sb, r1, r2, xs, xr,
    zo, zs, zt, zr, zxs, zxr, zacc, fin, finr,
    in_sem, y_send, y_recv, z_send, z_recv, c_send, c_recv,
):
    me_pw, me_pair = lax.axis_index("pw"), lax.axis_index("pair")
    y, z = me_pw % 4, me_pair // 4
    core = me_pair % 2
    y_next, y_prev, y_far = (y + 1) % 4, (y + 3) % 4, (y + 2) % 4
    z_next, z_prev, z_far = (z + 1) % 4, (z + 3) % 4, (z + 2) % 4
    x_hi = (me_pair // 2) % 2

    def along_y(t):
        return ((me_pw // 4) * 4 + t, me_pair)

    def along_z(t):
        return (me_pw, t * 4 + me_pair % 4)

    dev_yn, dev_yp = along_y(y_next), along_y(y_prev)
    dev_zn, dev_zp = along_z(z_next), along_z(z_prev)
    dev_x = ((me_pw + 4) % 8, me_pair)
    dev_xh = (me_pw, (me_pair // 4) * 4 + (me_pair + 2) % 4)
    dev_core = (me_pw, (me_pair // 2) * 2 + 1 - core)
    peers = (dev_yn, dev_yp, dev_zn, dev_zp, dev_x, dev_xh, dev_core)

    loads = [pltpu.make_async_copy(basis_hbm, basis, in_sem.at[0])]
    for c in range(NC):
        rows = pl.ds(c * CP, CP)
        loads.append(pltpu.make_async_copy(pw_hbm.at[rows], pw.at[rows], in_sem.at[1 + c]))
    for load in loads:
        load.start()

    barrier = pltpu.get_barrier_semaphore()
    for peer in peers:
        pl.semaphore_signal(barrier, inc=1, device_id=peer, device_id_type=MESH)

    sent = []

    def send(src, dst, s_sem, r_sem, dev):
        copy = pltpu.make_async_remote_copy(
            src_ref=src, dst_ref=dst, send_sem=s_sem, recv_sem=r_sem, device_id=dev, device_id_type=MESH
        )
        copy.start()
        sent.append(copy)

    def arrived(dst, sem):
        pltpu.make_async_copy(dst, dst, sem).wait()

    def quarter(t):
        return pl.multiple_of(t * BP, BP)

    def project(c):
        if c == 0:
            loads[0].wait()
        loads[1 + c].wait()

        def columns(n, carry):
            cols = pl.ds(pl.multiple_of(n * 256, 256), 256)
            part[c, :, cols] = jnp.dot(
                pw[pl.ds(c * CP, CP), :], basis[:, cols], preferred_element_type=F32
            ).astype(BF16)
            return carry

        lax.fori_loop(0, NB // 256, columns, 0)

    def y_first(c):
        far = quarter(y_far)
        send(part.at[c, pl.ds(far, HP)], ta.at[c], y_send.at[c, 0], y_recv.at[c, 0], dev_yn)
        send(part.at[c, pl.ds(far + HP, HP)], tb.at[c], y_send.at[c, 1], y_recv.at[c, 1], dev_yp)
        send(
            part.at[c, pl.ds(quarter(y_next) + HP, HP)], r1.at[c, pl.ds(HP, HP)],
            y_send.at[c, 2], y_recv.at[c, 2], dev_yn,
        )
        send(
            part.at[c, pl.ds(quarter(y_prev), HP)], r2.at[c, pl.ds(0, HP)],
            y_send.at[c, 3], y_recv.at[c, 3], dev_yp,
        )

    def y_second(c):
        arrived(ta.at[c], y_recv.at[c, 0])
        sa[c] = (ta[c].astype(F32) + part[c, pl.ds(quarter(y_next), HP), :].astype(F32)).astype(BF16)
        send(sa.at[c], r1.at[c, pl.ds(0, HP)], y_send.at[c, 4], y_recv.at[c, 4], dev_yn)
        arrived(tb.at[c], y_recv.at[c, 1])
        sb[c] = (tb[c].astype(F32) + part[c, pl.ds(quarter(y_prev) + HP, HP), :].astype(F32)).astype(BF16)
        send(sb.at[c], r2.at[c, pl.ds(HP, HP)], y_send.at[c, 5], y_recv.at[c, 5], dev_yp)

    def x_swap(c):
        arrived(r1.at[c, pl.ds(HP, HP)], y_recv.at[c, 2])
        arrived(r2.at[c, pl.ds(0, HP)], y_recv.at[c, 3])
        arrived(r1.at[c, pl.ds(0, HP)], y_recv.at[c, 4])
        arrived(r2.at[c, pl.ds(HP, HP)], y_recv.at[c, 5])
        xs[c] = (
            part[c, pl.ds(quarter(y), BP), :].astype(F32) + r1[c].astype(F32) + r2[c].astype(F32)
        ).astype(BF16)
        send(xs.at[c], xr.at[c], y_send.at[c, 6], y_recv.at[c, 6], dev_x)

    def to_core(c, start, size, k):
        send(
            cf.at[c, pl.ds(start, size)], cf.at[c, pl.ds(CP + start, size)],
            c_send.at[c, k], c_recv.at[c, k], dev_core,
        )

    def y_third(c):
        arrived(xr.at[c], y_recv.at[c, 6])
        mine = quarter(y)
        cf[c, pl.ds(mine, BP), :] = (xs[c].astype(F32) + xr[c].astype(F32)).astype(BF16)
        piece = cf.at[c, pl.ds(mine, BP)]
        send(piece, piece, y_send.at[c, 7], y_recv.at[c, 7], dev_yn)
        send(piece, piece, y_send.at[c, 8], y_recv.at[c, 8], dev_yp)
        to_core(c, mine, BP, 0)

    def y_fourth(c):
        before, after = quarter(y_prev), quarter(y_next)
        arrived(cf.at[c, pl.ds(before, BP)], y_recv.at[c, 7])
        half = cf.at[c, pl.ds(before, HP)]
        send(half, half, y_send.at[c, 9], y_recv.at[c, 9], dev_yn)
        arrived(cf.at[c, pl.ds(after, BP)], y_recv.at[c, 8])
        half = cf.at[c, pl.ds(after + HP, HP)]
        send(half, half, y_send.at[c, 10], y_recv.at[c, 10], dev_yp)
        to_core(c, before, BP, 1)
        to_core(c, after, BP, 2)

    def y_last(c):
        far = quarter(y_far)
        arrived(cf.at[c, pl.ds(far, HP)], y_recv.at[c, 9])
        arrived(cf.at[c, pl.ds(far + HP, HP)], y_recv.at[c, 10])
        to_core(c, far, BP, 3)

    def find_gaps():
        def occupied(e, value):
            return jnp.where(occ_ref[...] == e, oe_ref[e], value)

        def empty(e, value):
            return jnp.where(emp_ref[...] == e, ee_ref[e], value)

        zero = jnp.zeros((8, 128), F32)
        low = lax.fori_loop(0, 64, occupied, zero, unroll=8)
        high = lax.fori_loop(0, 256, empty, zero, unroll=8)
        gaps[0] = high - low

    def send_gaps():
        send(gaps.at[0], gaps.at[1], c_send.at[NC, 0], c_recv.at[NC, 0], dev_core)

    def find_factors():
        arrived(gaps.at[1], c_recv.at[NC, 0])
        for n in range(NW):
            frequency = fg_ref[fi_ref[core * NW + n]]
            for src in range(2):
                gap = gaps[src]
                below, above = frequency - gap, frequency + gap
                fac[src, n] = (4.0 / PAIRS) * (
                    below / (below * below + broadening_sq) - above / (above * above + broadening_sq)
                )

    def weigh(c):
        y_core = [(mine, BP, 0) for mine in (quarter(y),)]
        y_core += [(quarter(y_prev), BP, 1), (quarter(y_next), BP, 2), (quarter(y_far), BP, 3)]
        for start, size, k in y_core:
            arrived(cf.at[c, pl.ds(CP + start, size)], c_recv.at[c, k])
        rows = pl.ds(pl.multiple_of(me_pw * ROWS, ROWS), ROWS)
        for src in range(2):
            for r in range(CP // 128):
                first = src * CP + r * 128
                block = cf[c, pl.ds(first, 128), rows].astype(F32).T

                def one(n, carry):
                    row = fac[src, n, pl.ds(c * (CP // 128) + r, 1), :]
                    wt[pl.ds(pl.multiple_of(n * ROWS, ROWS), ROWS), pl.ds(first, 128)] = (
                        block * row
                    ).astype(BF16)
                    return carry

                lax.fori_loop(0, NW, one, 0, unroll=2)

    def tiles(c, q):
        rows = pl.ds(pl.multiple_of(q * QR, QR), QR)
        value = jnp.dot(wt[rows, :], cf[c], preferred_element_type=F32)
        if c:
            value = acc[rows, :] + value
        acc[rows, :] = value

    def all_tiles(c):
        def group(q, carry):
            tiles(c, q)
            return carry

        lax.fori_loop(0, NQ, group, 0)

    def zcols(t):
        return pl.ds(pl.multiple_of(t * ZC, ZC), ZC)

    def half_a(q):
        return pl.ds(q * QR, ROWS)

    def half_b(q):
        return pl.ds(q * QR + ROWS, ROWS)

    def z_first(q):
        a, b = half_a(q), half_b(q)
        zo[q, 0] = acc[a, zcols(z_far)].astype(BF16)
        send(zo.at[q, 0], zt.at[q, 0], z_send.at[q, 0], z_recv.at[q, 0], dev_zn)
        zo[q, 1] = acc[b, zcols(z_far)].astype(BF16)
        send(zo.at[q, 1], zt.at[q, 1], z_send.at[q, 1], z_recv.at[q, 1], dev_zp)
        zo[q, 2] = acc[b, zcols(z_next)].astype(BF16)
        send(zo.at[q, 2], zr.at[q, 2], z_send.at[q, 2], z_recv.at[q, 2], dev_zn)
        zo[q, 3] = acc[a, zcols(z_prev)].astype(BF16)
        send(zo.at[q, 3], zr.at[q, 3], z_send.at[q, 3], z_recv.at[q, 3], dev_zp)

    def z_second(q):
        a, b = half_a(q), half_b(q)
        arrived(zt.at[q, 0], z_recv.at[q, 0])
        zs[q, 0] = (acc[a, zcols(z_next)] + zt[q, 0].astype(F32)).astype(BF16)
        send(zs.at[q, 0], zr.at[q, 0], z_send.at[q, 4], z_recv.at[q, 4], dev_zn)
        arrived(zt.at[q, 1], z_recv.at[q, 1])
        zs[q, 1] = (acc[b, zcols(z_prev)] + zt[q, 1].astype(F32)).astype(BF16)
        send(zs.at[q, 1], zr.at[q, 1], z_send.at[q, 5], z_recv.at[q, 5], dev_zp)

    def x_last(q):
        arrived(zr.at[q, 2], z_recv.at[q, 2])
        arrived(zr.at[q, 3], z_recv.at[q, 3])
        arrived(zr.at[q, 0], z_recv.at[q, 4])
        arrived(zr.at[q, 1], z_recv.at[q, 5])
        here = pl.multiple_of(x_hi * XC, XC)
        there = pl.multiple_of((1 - x_hi) * XC, XC)
        base = pl.multiple_of(z * ZC, ZC)

        def total(half, rows, first, second, cols):
            return (
                acc[rows, pl.ds(base + cols, XC)]
                + zr[q, first, :, pl.ds(cols, XC)].astype(F32)
                + zr[q, second, :, pl.ds(cols, XC)].astype(F32)
            )

        zxs[q, 0] = total(0, half_a(q), 0, 3, there).astype(BF16)
        zxs[q, 1] = total(1, half_b(q), 2, 1, there).astype(BF16)
        send(zxs.at[q], zxr.at[q], z_send.at[q, 6], z_recv.at[q, 6], dev_xh)
        zacc[q, 0] = total(0, half_a(q), 0, 3, here)
        zacc[q, 1] = total(1, half_b(q), 2, 1, here)

    def finish(q):
        arrived(zxr.at[q], z_recv.at[q, 6])
        for h in range(2):
            fin[2 * q + h] = (zacc[q, h] + zxr[q, h].astype(F32)).T
        theirs = pl.ds(pl.multiple_of((1 - core) * 64, 64), 64)
        send(
            fin.at[pl.ds(2 * q, 2), theirs, :], finr.at[pl.ds(2 * q, 2)],
            z_send.at[q, 7], z_recv.at[q, 7], dev_core,
        )
        mine = pl.ds(pl.multiple_of(core * 64, 64), 64)
        out_ref[pl.ds(core * NW + 2 * q, 2)] = fin[pl.ds(2 * q, 2), mine, :]

    def take(q):
        arrived(finr.at[pl.ds(2 * q, 2)], z_recv.at[q, 7])
        out_ref[pl.ds((1 - core) * NW + 2 * q, 2)] = finr[pl.ds(2 * q, 2)]

    project(0)
    pl.semaphore_wait(barrier, len(peers))
    y_first(0)
    project(1)
    y_first(1)
    y_second(0)
    project(2)
    y_first(2)
    y_second(1)
    x_swap(0)
    project(3)
    y_first(3)
    y_second(2)
    x_swap(1)
    y_third(0)
    find_gaps()
    send_gaps()
    y_second(3)
    x_swap(2)
    y_third(1)
    y_fourth(0)
    find_factors()
    x_swap(3)
    y_third(2)
    y_fourth(1)
    y_last(0)
    y_third(3)
    weigh(0)
    all_tiles(0)
    y_fourth(2)
    y_last(1)
    y_fourth(3)
    weigh(1)
    all_tiles(1)
    y_last(2)
    weigh(2)
    all_tiles(2)
    y_last(3)
    weigh(3)
    for q in range(NQ):
        tiles(3, q)
        z_first(q)
        if q >= 1:
            z_second(q - 1)
        if q >= 2:
            x_last(q - 2)
    z_second(NQ - 1)
    x_last(NQ - 2)
    finish(0)
    x_last(NQ - 1)
    for q in range(1, NQ):
        finish(q)
    for q in range(NQ):
        take(q)
    for copy in sent:
        copy.wait_send()


def on_device(pair_waves, subspace_basis, occ_band, empty_band, occ_energy, empty_energy, freq_grid, freq_index):
    vmem = pl.BlockSpec(memory_space=pltpu.VMEM)
    smem = pl.BlockSpec(memory_space=pltpu.SMEM)
    hbm = pl.BlockSpec(memory_space=pl.ANY)
    dma = pltpu.SemaphoreType.DMA
    out = pl.pallas_call(
        kernel,
        out_shape=jax.ShapeDtypeStruct((NFREQ, 64, ROWS), F32),
        in_specs=[vmem, vmem, hbm, hbm, smem, smem, smem, smem],
        out_specs=vmem,
        scratch_shapes=[
            pltpu.VMEM((PL, PWL), BF16),
            pltpu.VMEM((PWL, NB), BF16),
            pltpu.VMEM((NC, CP, NB), BF16),
            pltpu.VMEM((NC, 2 * CP, NB), BF16),
            pltpu.VMEM((NW * ROWS, NB), F32),
            pltpu.VMEM((NW * ROWS, 2 * CP), BF16),
            pltpu.VMEM((2, 8, 128), F32),
            pltpu.VMEM((2, NW, 8, 128), F32),
            pltpu.VMEM((NC, HP, NB), BF16),
            pltpu.VMEM((NC, HP, NB), BF16),
            pltpu.VMEM((NC, HP, NB), BF16),
            pltpu.VMEM((NC, HP, NB), BF16),
            pltpu.VMEM((NC, BP, NB), BF16),
            pltpu.VMEM((NC, BP, NB), BF16),
            pltpu.VMEM((NC, BP, NB), BF16),
            pltpu.VMEM((NC, BP, NB), BF16),
            pltpu.VMEM((NQ, 4, ROWS, ZC), BF16),
            pltpu.VMEM((NQ, 2, ROWS, ZC), BF16),
            pltpu.VMEM((NQ, 2, ROWS, ZC), BF16),
            pltpu.VMEM((NQ, 4, ROWS, ZC), BF16),
            pltpu.VMEM((NQ, 2, ROWS, XC), BF16),
            pltpu.VMEM((NQ, 2, ROWS, XC), BF16),
            pltpu.VMEM((NQ, 2, ROWS, XC), F32),
            pltpu.VMEM((NW, ROWS, ROWS), F32),
            pltpu.VMEM((NW, 64, ROWS), F32),
            dma((1 + NC,)),
            dma((NC, 11)),
            dma((NC, 11)),
            dma((NQ, 8)),
            dma((NQ, 8)),
            dma((NC + 1, 4)),
            dma((NC + 1, 4)),
        ],
        compiler_params=pltpu.CompilerParams(collective_id=0, has_side_effects=True),
        cost_estimate=pl.CostEstimate(flops=9 << 30, bytes_accessed=9 << 20, transcendentals=0),
    )(
        occ_band.reshape(8, 128), empty_band.reshape(8, 128), pair_waves, subspace_basis,
        occ_energy, empty_energy, freq_grid, freq_index,
    )
    return jnp.swapaxes(out, 1, 2)


def solution(mesh):
    return jax.shard_map(
        on_device,
        mesh=mesh,
        in_specs=(P("pair", "pw"), P("pw", None), P("pair"), P("pair"), P(), P(), P(), P()),
        out_specs=P(None, "pw", "pair"),
        check_vma=False,
    )
```

time: 176 us -> 81.9 us (0.47)
  blocking collectives: 110 us -> 0 us
  Pallas kernels: 0 us -> 79.8 us
  matrix products: 29.5 us -> 0 us
  between operations: 13.6 us -> 0.01 us
  starting transfers between devices: 11.4 us -> 0 us
  other arithmetic: 4.95 us -> 0 us
  local copies, waits for them, and re-layouts: 6.6 us -> 1.89 us
    pallas_call x0 -> x1, Pallas kernels: none -> 79.8 us  [on_device(): pl.pallas_call(kernel, out_shape=jax.ShapeDtypeStruct((NFREQ, 64, ROWS),...]
    all_to_all x2 -> x0, blocking collectives: 61.7 us -> none  [the longest x1 31.5 us: sent_and_summed(): lax.all_to_all(parts, axis, split_axis=0, concat_axis=0, tiled=True)]
    all_gather x1 -> x0, blocking collectives: 48.2 us -> none  [on_device(): lax.all_gather(factor.astype(jnp.bfloat16), 'pair', axis=1, tiled=True)]
    dot_general x2 -> x0, matrix products: 29.5 us -> none  [the longest x1 21.5 us: on_device(): jnp.einsum('fsp,tp->fst', weighted, col_all, preferred_element_type=jnp.f...]
    all_to_all x1 -> x0, starting transfers between devices: 11.4 us -> none  [on_device(): lax.all_to_all(projected, 'pair', split_axis=0, concat_axis=1, tiled=True)]
    all_to_all x2 -> x0, local copies, waits for them, and re-layouts: 5.36 us -> none  [on_device(): lax.all_to_all(projected, 'pair', split_axis=0, concat_axis=1, tiled=True)]
    convert_element_type x3 -> x0, other arithmetic: 3.2 us -> none  [the longest x1 3.02 us: on_device(): rows_piece.astype(jnp.float32)[None, :, :] * factor_piece[:, None, :]]
    unnamed x12 -> x1, local copies, waits for them, and re-layouts: 0.04 us -> 1.89 us
  transfers between devices with their start and end apart: 2 -> 0, of which waited for: 0 -> 0; matrix products, arithmetic and copies ran while one was open for 4% -> 0% of each run, Pallas kernels for 0% -> 0%
where the time goes in v1:
time: 81.9 us; the launch traced here: 81.7 us
  Pallas kernels  79.8 us (97%)
  local copies, waits for them, and re-layouts  1.89 us (2%)
    pallas_call x1, Pallas kernels, on_device(): pl.pallas_call(kernel, out_shape=jax.ShapeDtypeStruct((NFREQ, 64, ROWS),...  79.8 us
    unnamed x1, local copies, waits for them, and re-layouts  1.89 us

profile of v1, /device:TPU:1, one launch (start us, length us, event | category | flops | bytes accessed | tf_op | source)
XLA Modules:
  0.0 81.7 jit_solution(13882578109293838927)
XLA Ops:
  0.0 79.8 %shard_map.82 = f32[16,64,128]{2,1,0:T(8,128)} custom-call(s32[8,128]{1,0:T(8,128)} %bitcast.4, s32[8,128]{1,0:T(8,128)} %bitcast.5, bf16[1024,2048]{1,0:T(8,128)(2,1)} %pw_hbm.1, bf16[2048,1024]{1,0:T(8,128)(2,1)} %basis_hbm.1, f32[64]{0:T(128)} %oe_ref.1, f32[256]{0:T(256)} %ee_ref.1, f32[16]{0:T(128)} %fg_ref.1, s32[16]{0:T(128)} %fi_ref.1), custom_call_target="tpu_custom_call" | custom-call | flops 9663676416 | bytes 9437184 | tf_op jit(solution)/shard_map/pallas_call | solution.py:349
  79.8 1.9 %copy.10 = f32[16,128,64]{1,2,0:T(8,128)} copy(f32[16,128,64]{1,2,0:T(8,128)} %bitcast.3) | data formatting | bytes 1048576

commit v2 on v0

v2 whole, which is shorter than its diff:
```python
import jax
import jax.numpy as jnp
from jax import lax
from jax.experimental import pallas as pl
from jax.experimental.pallas import tpu as pltpu
from jax.sharding import PartitionSpec as P

F32, BF16 = jnp.float32, jnp.bfloat16
MESH = pl.DeviceIdType.MESH
broadening_sq = 0.0025

PAIRS = 16384
NFREQ = 16
NW = 8
NB = 1024
PL = 1024
PWL = 2048
ROWS = 128
BC = 256
NC = 8
CP = PL // NC
HP = CP // 2
NG = 4
GP = PL // NG
GC = NC // NG
NQ = 4
QR = NW * ROWS // NQ
OWN, NEXT, FAR, PREV = range(4)


def kernel(
    occ_ref, emp_ref, pw_hbm, basis_hbm, oe_ref, ee_ref, fg_ref, fi_ref, out_ref,
    pw, basis, part, cf, wt, gaps, fac,
    tab, sab, r12, xs, xr,
    val, zo, zs, zt, zr, zxs, zxr, zacc, fin, finr,
    load_sem, send_sem, y_recv, g_recv, z_recv, x_recv, c_recv,
):
    me_pw, me_pair = lax.axis_index("pw"), lax.axis_index("pair")
    x_lo, y = me_pw // 4, me_pw % 4
    z, x_hi, core = me_pair // 4, (me_pair // 2) % 2, me_pair % 2
    ys = [(y + d) % 4 for d in range(4)]
    z_next, z_prev, z_far = (z + 1) % 4, (z + 3) % 4, (z + 2) % 4

    def along_y(t):
        return (x_lo * 4 + t, me_pair)

    def along_z(t):
        return (me_pw, t * 4 + me_pair % 4)

    dev_yn, dev_yp = along_y(ys[NEXT]), along_y(ys[PREV])
    dev_zn, dev_zp = along_z(z_next), along_z(z_prev)
    dev_x = ((me_pw + 4) % 8, me_pair)
    dev_xh = (me_pw, z * 4 + (me_pair + 2) % 4)
    dev_core = (me_pw, (me_pair // 2) * 2 + 1 - core)
    peers = (dev_yn, dev_yp, dev_zn, dev_zp, dev_x, dev_xh, dev_core)

    def chunk(c):
        return pl.ds(c * CP, CP)

    def half(c, h):
        return pl.ds(c * CP + h * HP, HP)

    def group(g):
        return pl.ds(g * GP, GP)

    def group_half(g, h):
        return pl.ds(g * GP + h * (GP // 2), GP // 2)

    pw_loads = [pltpu.make_async_copy(pw_hbm.at[group(g)], pw.at[group(g)], load_sem.at[g]) for g in range(NG)]
    pw_loads[0].start()
    for d in (FAR, NEXT, PREV, OWN):
        for l in range(2):
            pltpu.make_async_copy(
                basis_hbm.at[:, pl.ds(pl.multiple_of(l * 512 + ys[d] * 128, 128), 128)],
                basis.at[ys[d], :, pl.ds(l * 128, 128)],
                load_sem.at[NG + d],
            ).start()
    for load in pw_loads[1:]:
        load.start()

    barrier = pltpu.get_barrier_semaphore()
    for peer in peers:
        pl.semaphore_signal(barrier, inc=1, device_id=peer, device_id_type=MESH)

    def remote(src, dst, s_sem, r_sem, dev):
        return pltpu.make_async_remote_copy(
            src_ref=src, dst_ref=dst, send_sem=s_sem, recv_sem=r_sem, device_id=dev, device_id_type=MESH
        )

    y_sent, c_sent, gap_sent = send_sem.at[0], send_sem.at[1], send_sem.at[2]

    def arrived(dst, sem):
        pltpu.make_async_copy(dst, dst, sem).wait()

    def project(g, d):
        if d == FAR:
            pw_loads[g].wait()
        if g == 0:
            arrived(basis.at[ys[d]], load_sem.at[NG + d])
        part[ys[d], group(g), :] = jnp.dot(
            pw[group(g), :], basis[ys[d]], preferred_element_type=F32
        ).astype(BF16)

    def chunks(g):
        return range(g * GC, (g + 1) * GC)

    def y_far(g):
        for c in chunks(g):
            remote(part.at[ys[FAR], half(c, 0)], tab.at[c, 0], y_sent, y_recv.at[c, 0], dev_yn).start()
            remote(part.at[ys[FAR], half(c, 1)], tab.at[c, 1], y_sent, y_recv.at[c, 0], dev_yp).start()

    def y_near(g):
        project(g, NEXT)
        for c in chunks(g):
            remote(
                part.at[ys[NEXT], half(c, 1)], r12.at[c, 0, pl.ds(HP, HP)], y_sent, y_recv.at[c, 1], dev_yn
            ).start()
        project(g, PREV)
        for c in chunks(g):
            remote(
                part.at[ys[PREV], half(c, 0)], r12.at[c, 1, pl.ds(0, HP)], y_sent, y_recv.at[c, 1], dev_yp
            ).start()

    def y_second(g):
        for c in chunks(g):
            arrived(tab.at[c], y_recv.at[c, 0])
            sab[c, 0] = (tab[c, 0].astype(F32) + part[ys[NEXT], half(c, 0), :].astype(F32)).astype(BF16)
            remote(sab.at[c, 0], r12.at[c, 0, pl.ds(0, HP)], y_sent, y_recv.at[c, 1], dev_yn).start()
            sab[c, 1] = (tab[c, 1].astype(F32) + part[ys[PREV], half(c, 1), :].astype(F32)).astype(BF16)
            remote(sab.at[c, 1], r12.at[c, 1, pl.ds(HP, HP)], y_sent, y_recv.at[c, 1], dev_yp).start()

    def x_swap(c):
        arrived(r12.at[c], y_recv.at[c, 1])
        xs[c] = (
            part[ys[OWN], chunk(c), :].astype(F32) + r12[c, 0].astype(F32) + r12[c, 1].astype(F32)
        ).astype(BF16)
        remote(xs.at[c], xr.at[c], y_sent, y_recv.at[c, 2], dev_x).start()

    def to_core(g, d):
        sem = c_recv.at[g] if d == OWN else c_recv.at[NG + d - 1]
        remote(cf.at[ys[d], group(g)], cf.at[ys[d], pl.ds(PL + g * GP, GP)], c_sent, sem, dev_core).start()

    def from_core(d):
        arrived(cf.at[ys[d], pl.ds(PL, PL)], c_recv.at[NG + d - 1])

    def y_third(g):
        for c in chunks(g):
            arrived(xr.at[c], y_recv.at[c, 2])
            cf[ys[OWN], chunk(c), :] = (xs[c].astype(F32) + xr[c].astype(F32)).astype(BF16)
        piece = cf.at[ys[OWN], group(g)]
        remote(piece, piece, y_sent, g_recv.at[g, 0], dev_yn).start()
        remote(piece, piece, y_sent, g_recv.at[g, 1], dev_yp).start()
        to_core(g, OWN)

    def y_fourth(g):
        arrived(cf.at[ys[PREV], group(g)], g_recv.at[g, 0])
        piece = cf.at[ys[PREV], group_half(g, 0)]
        remote(piece, piece, y_sent, g_recv.at[g, 2], dev_yn).start()
        arrived(cf.at[ys[NEXT], group(g)], g_recv.at[g, 1])
        piece = cf.at[ys[NEXT], group_half(g, 1)]
        remote(piece, piece, y_sent, g_recv.at[g, 2], dev_yp).start()
        to_core(g, PREV)
        to_core(g, NEXT)

    def y_last(g):
        arrived(cf.at[ys[FAR], group(g)], g_recv.at[g, 2])
        to_core(g, FAR)

    def find_gaps():
        def occupied(e, value):
            return jnp.where(occ_ref[...] == e, oe_ref[e], value)

        def empty(e, value):
            return jnp.where(emp_ref[...] == e, ee_ref[e], value)

        zero = jnp.zeros((8, 128), F32)
        low = lax.fori_loop(0, 64, occupied, zero, unroll=8)
        high = lax.fori_loop(0, 256, empty, zero, unroll=8)
        gaps[0] = high - low

    def send_gaps():
        remote(gaps.at[0], gaps.at[1], gap_sent, c_recv.at[NG + 3], dev_core).start()

    def find_factors():
        arrived(gaps.at[1], c_recv.at[NG + 3])
        for n in range(NW):
            frequency = fg_ref[fi_ref[core * NW + n]]
            for src in range(2):
                gap = gaps[src]
                below, above = frequency - gap, frequency + gap
                fac[src, n] = (4.0 / PAIRS) * (
                    below / (below * below + broadening_sq) - above / (above * above + broadening_sq)
                )

    def weigh(g):
        arrived(cf.at[ys[OWN], pl.ds(PL + g * GP, GP)], c_recv.at[g])
        rows = pl.ds(pl.multiple_of(x_lo * ROWS, ROWS), ROWS)
        for src in range(2):
            for r in range(GP // 128):
                first = src * PL + g * GP + r * 128
                block = cf[ys[OWN], pl.ds(first, 128), rows].astype(F32).T

                def one(n, carry):
                    row = fac[src, n, pl.ds(g * (GP // 128) + r, 1), :]
                    wt[pl.ds(pl.multiple_of(n * ROWS, ROWS), ROWS), pl.ds(first, 128)] = (
                        block * row
                    ).astype(BF16)
                    return carry

                lax.fori_loop(0, NW, one, 0, unroll=2)

    slot = [ys[d] % 2 for d in range(4)]
    root = [(z % 2) == ys[d] // 2 for d in range(4)]
    here, there = pl.ds(0, ROWS), pl.ds(ROWS, ROWS)

    def cols(t):
        return pl.ds(pl.multiple_of((t // 2) * 128, 128), 128)

    def tiles(d, q):
        val[d, q] = jnp.dot(wt[pl.ds(q * QR, QR), :], cf[ys[d]], preferred_element_type=F32)

        @pl.when(root[d])
        def _():
            zo[d, q, 0] = val[d, q, here, cols(z_far)].astype(BF16)
            remote(zo.at[d, q, 0], zt.at[slot[d], q, 0], c_sent, z_recv.at[d, q], dev_zn).start()
            zo[d, q, 1] = val[d, q, there, cols(z_far)].astype(BF16)
            remote(zo.at[d, q, 1], zt.at[slot[d], q, 1], c_sent, z_recv.at[d, q], dev_zp).start()

        @pl.when(jnp.logical_not(root[d]))
        def _():
            zo[d, q, 0] = val[d, q, there, cols(z_next)].astype(BF16)
            remote(zo.at[d, q, 0], zr.at[slot[d], q, 2], c_sent, z_recv.at[d, q], dev_zn).start()
            zo[d, q, 1] = val[d, q, here, cols(z_prev)].astype(BF16)
            remote(zo.at[d, q, 1], zr.at[slot[d], q, 3], c_sent, z_recv.at[d, q], dev_zp).start()

    def z_second(d, q):
        @pl.when(jnp.logical_not(root[d]))
        def _():
            arrived(zt.at[slot[d], q], z_recv.at[d, q])
            zs[slot[d], q, 0] = (val[d, q, here, cols(z_next)] + zt[slot[d], q, 0].astype(F32)).astype(BF16)
            remote(zs.at[slot[d], q, 0], zr.at[slot[d], q, 0], c_sent, z_recv.at[d, q], dev_zn).start()
            zs[slot[d], q, 1] = (val[d, q, there, cols(z_prev)] + zt[slot[d], q, 1].astype(F32)).astype(BF16)
            remote(zs.at[slot[d], q, 1], zr.at[slot[d], q, 1], c_sent, z_recv.at[d, q], dev_zp).start()

    def z_third(d, q):
        @pl.when(root[d])
        def _():
            arrived(zr.at[slot[d], q], z_recv.at[d, q])

            def total(rows, first, second):
                return (
                    val[d, q, rows, cols(z)]
                    + zr[slot[d], q, first].astype(F32)
                    + zr[slot[d], q, second].astype(F32)
                )

            @pl.when(slot[d] == x_hi)
            def _():
                zacc[q, 0] = total(here, 0, 3)
                zacc[q, 1] = total(there, 2, 1)

            @pl.when(slot[d] != x_hi)
            def _():
                zxs[q, 0] = total(here, 0, 3).astype(BF16)
                zxs[q, 1] = total(there, 2, 1).astype(BF16)
                remote(zxs.at[q], zxr.at[q], c_sent, x_recv.at[q, 0], dev_xh).start()

    def finish(q):
        arrived(zxr.at[q], x_recv.at[q, 0])
        for h in range(2):
            fin[2 * q + h] = (zacc[q, h] + zxr[q, h].astype(F32)).T
        theirs = pl.ds(pl.multiple_of((1 - core) * 64, 64), 64)
        remote(
            fin.at[pl.ds(2 * q, 2), theirs, :], finr.at[pl.ds(2 * q, 2)], c_sent, x_recv.at[q, 1], dev_core
        ).start()
        mine = pl.ds(pl.multiple_of(core * 64, 64), 64)
        out_ref[pl.ds(core * NW + 2 * q, 2)] = fin[pl.ds(2 * q, 2), mine, :]

    def take(q):
        arrived(finr.at[pl.ds(2 * q, 2)], x_recv.at[q, 1])
        out_ref[pl.ds((1 - core) * NW + 2 * q, 2)] = finr[pl.ds(2 * q, 2)]

    project(0, FAR)
    pl.semaphore_wait(barrier, len(peers))
    y_far(0)
    project(1, FAR)
    y_far(1)
    y_near(0)
    y_second(0)
    project(2, FAR)
    y_far(2)
    y_near(1)
    y_second(1)
    project(3, FAR)
    y_far(3)
    y_near(2)
    project(0, OWN)
    x_swap(0)
    x_swap(1)
    y_second(2)
    y_near(3)
    project(1, OWN)
    x_swap(2)
    x_swap(3)
    project(2, OWN)
    y_second(3)
    y_third(0)
    project(3, OWN)
    find_gaps()
    send_gaps()
    x_swap(4)
    x_swap(5)
    y_third(1)
    find_factors()
    weigh(0)
    x_swap(6)
    x_swap(7)
    y_third(2)
    weigh(1)
    y_third(3)
    weigh(2)
    weigh(3)
    y_fourth(0)
    y_fourth(1)
    for q in range(NQ):
        tiles(OWN, q)
    y_fourth(2)
    y_fourth(3)
    from_core(NEXT)
    for q in range(NQ):
        z_second(OWN, q)
        tiles(NEXT, q)
    from_core(PREV)
    y_last(0)
    y_last(1)
    for q in range(NQ):
        z_third(OWN, q)
        z_second(NEXT, q)
        tiles(PREV, q)
    y_last(2)
    y_last(3)
    from_core(FAR)
    for q in range(NQ):
        z_second(PREV, q)
        tiles(FAR, q)
    for q in range(NQ):
        z_third(NEXT, q)
    for q in range(NQ):
        z_second(FAR, q)
        z_third(PREV, q)
    for q in range(NQ):
        z_third(FAR, q)
    for q in range(NQ):
        finish(q)
    for q in range(NQ):
        take(q)
    arrived(pw.at[pl.ds(0, 896)], y_sent)
    arrived(pw, c_sent)
    arrived(gaps.at[0], gap_sent)


def on_device(pair_waves, subspace_basis, occ_band, empty_band, occ_energy, empty_energy, freq_grid, freq_index):
    vmem = pl.BlockSpec(memory_space=pltpu.VMEM)
    smem = pl.BlockSpec(memory_space=pltpu.SMEM)
    hbm = pl.BlockSpec(memory_space=pl.ANY)
    dma = pltpu.SemaphoreType.DMA
    out = pl.pallas_call(
        kernel,
        out_shape=jax.ShapeDtypeStruct((NFREQ, 64, ROWS), F32),
        in_specs=[vmem, vmem, hbm, hbm, smem, smem, smem, smem],
        out_specs=vmem,
        scratch_shapes=[
            pltpu.VMEM((PL, PWL), BF16),
            pltpu.VMEM((4, PWL, BC), BF16),
            pltpu.VMEM((4, PL, BC), BF16),
            pltpu.VMEM((4, 2 * PL, BC), BF16),
            pltpu.VMEM((NW * ROWS, 2 * PL), BF16),
            pltpu.VMEM((2, 8, 128), F32),
            pltpu.VMEM((2, NW, 8, 128), F32),
            pltpu.VMEM((NC, 2, HP, BC), BF16),
            pltpu.VMEM((NC, 2, HP, BC), BF16),
            pltpu.VMEM((NC, 2, CP, BC), BF16),
            pltpu.VMEM((NC, CP, BC), BF16),
            pltpu.VMEM((NC, CP, BC), BF16),
            pltpu.VMEM((4, NQ, QR, BC), F32),
            pltpu.VMEM((4, NQ, 2, ROWS, ROWS), BF16),
            pltpu.VMEM((2, NQ, 2, ROWS, ROWS), BF16),
            pltpu.VMEM((2, NQ, 2, ROWS, ROWS), BF16),
            pltpu.VMEM((2, NQ, 4, ROWS, ROWS), BF16),
            pltpu.VMEM((NQ, 2, ROWS, ROWS), BF16),
            pltpu.VMEM((NQ, 2, ROWS, ROWS), BF16),
            pltpu.VMEM((NQ, 2, ROWS, ROWS), F32),
            pltpu.VMEM((NW, ROWS, ROWS), F32),
            pltpu.VMEM((NW, 64, ROWS), F32),
            dma((NG + 4,)),
            dma((3,)),
            dma((NC, 3)),
            dma((NG, 3)),
            dma((4, NQ)),
            dma((NQ, 2)),
            dma((NG + 4,)),
        ],
        compiler_params=pltpu.CompilerParams(collective_id=0, has_side_effects=True),
        cost_estimate=pl.CostEstimate(flops=9 << 30, bytes_accessed=9 << 20, transcendentals=0),
    )(
        occ_band.reshape(8, 128), empty_band.reshape(8, 128), pair_waves, subspace_basis,
        occ_energy, empty_energy, freq_grid, freq_index,
    )
    return jnp.swapaxes(out, 1, 2)


def solution(mesh):
    return jax.shard_map(
        on_device,
        mesh=mesh,
        in_specs=(P("pair", "pw"), P("pw", None), P("pair"), P("pair"), P(), P(), P(), P()),
        out_specs=P(None, "pw", "pair"),
        check_vma=False,
    )
```

time: 176 us -> 71.3 us (0.41)
  the two profiles are of different devices: /device:TPU:1 before, /device:TPU:33 now
where the time goes in v2:
time: 71.3 us; the launch traced here: 71.1 us
  Pallas kernels  69.2 us (97%)
  local copies, waits for them, and re-layouts  1.89 us (3%)
    pallas_call x1, Pallas kernels, on_device(): pl.pallas_call(kernel, out_shape=jax.ShapeDtypeStruct((NFREQ, 64, ROWS),...  69.2 us
    unnamed x1, local copies, waits for them, and re-layouts  1.89 us

profile of v2, /device:TPU:33, one launch (start us, length us, event | category | flops | bytes accessed | tf_op | source)
XLA Modules:
  0.0 71.1 jit_solution(3103874463094459336)
XLA Ops:
  0.0 69.2 %shard_map.82 = f32[16,64,128]{2,1,0:T(8,128)} custom-call(s32[8,128]{1,0:T(8,128)} %bitcast.4, s32[8,128]{1,0:T(8,128)} %bitcast.5, bf16[1024,2048]{1,0:T(8,128)(2,1)} %pw_hbm.1, bf16[2048,1024]{1,0:T(8,128)(2,1)} %basis_hbm.1, f32[64]{0:T(128)} %oe_ref.1, f32[256]{0:T(256)} %ee_ref.1, f32[16]{0:T(128)} %fg_ref.1, s32[16]{0:T(128)} %fi_ref.1), custom_call_target="tpu_custom_call" | custom-call | flops 9663676416 | bytes 9437184 | tf_op jit(solution)/shard_map/pallas_call | solution.py:367
  69.2 1.9 %copy.10 = f32[16,128,64]{1,2,0:T(8,128)} copy(f32[16,128,64]{1,2,0:T(8,128)} %bitcast.3) | data formatting | bytes 1048576

commit v3 on v2

--- a/solution.py
+++ b/solution.py
@@ -31,9 +31,9 @@
 def kernel(
     occ_ref, emp_ref, pw_hbm, basis_hbm, oe_ref, ee_ref, fg_ref, fi_ref, out_ref,
     pw, basis, part, cf, wt, gaps, fac,
-    tab, sab, r12, xs, xr,
-    val, zo, zs, zt, zr, zxs, zxr, zacc, fin, finr,
-    load_sem, send_sem, y_recv, g_recv, z_recv, x_recv, c_recv,
+    hx, hs, tab, sab, r12, xs, xr,
+    val, zo, zs, zt, zr, zxs, zxr, fin, finr,
+    load_sem, send_sem, y_recv, g_recv, h_recv, z_recv, x_recv, c_recv,
 ):
     me_pw, me_pair = lax.axis_index("pw"), lax.axis_index("pair")
     x_lo, y = me_pw // 4, me_pw % 4
@@ -51,8 +51,9 @@
     dev_zn, dev_zp = along_z(z_next), along_z(z_prev)
     dev_x = ((me_pw + 4) % 8, me_pair)
     dev_xh = (me_pw, z * 4 + (me_pair + 2) % 4)
+    dev_xhc = (me_pw, z * 4 + ((me_pair // 2) * 2 + 3 - core) % 4)
     dev_core = (me_pw, (me_pair // 2) * 2 + 1 - core)
-    peers = (dev_yn, dev_yp, dev_zn, dev_zp, dev_x, dev_xh, dev_core)
+    peers = (dev_yn, dev_yp, dev_zn, dev_zp, dev_x, dev_xh, dev_xhc, dev_core)
 
     def chunk(c):
         return pl.ds(c * CP, CP)
@@ -67,16 +68,22 @@
         return pl.ds(g * GP + h * (GP // 2), GP // 2)
 
     pw_loads = [pltpu.make_async_copy(pw_hbm.at[group(g)], pw.at[group(g)], load_sem.at[g]) for g in range(NG)]
-    pw_loads[0].start()
-    for d in (FAR, NEXT, PREV, OWN):
+    def load_basis(d):
         for l in range(2):
             pltpu.make_async_copy(
                 basis_hbm.at[:, pl.ds(pl.multiple_of(l * 512 + ys[d] * 128, 128), 128)],
                 basis.at[ys[d], :, pl.ds(l * 128, 128)],
                 load_sem.at[NG + d],
             ).start()
-    for load in pw_loads[1:]:
-        load.start()
+
+    load_basis(FAR)
+    pw_loads[1].start()
+    pw_loads[0].start()
+    load_basis(NEXT)
+    load_basis(PREV)
+    pw_loads[2].start()
+    pw_loads[3].start()
+    load_basis(OWN)
 
     barrier = pltpu.get_barrier_semaphore()
     for peer in peers:
@@ -95,7 +102,7 @@
     def project(g, d):
         if d == FAR:
             pw_loads[g].wait()
-        if g == 0:
+        if g == 1:
             arrived(basis.at[ys[d]], load_sem.at[NG + d])
         part[ys[d], group(g), :] = jnp.dot(
             pw[group(g), :], basis[ys[d]], preferred_element_type=F32
@@ -104,37 +111,110 @@
     def chunks(g):
         return range(g * GC, (g + 1) * GC)
 
-    def y_far(g):
+    def mine(c, d):
+        return hs.at[ys[d]] if c == 0 else part.at[ys[d], chunk(c)]
+
+    kept = pl.ds(pl.multiple_of(x_lo * CP, CP), CP)
+    given = pl.ds(pl.multiple_of((1 - x_lo) * CP, CP), CP)
+
+    def x_give(d):
+        project(0, d)
+        remote(part.at[ys[d], given], hx.at[ys[d]], y_sent, h_recv.at[0, d], dev_x).start()
+
+    def x_take(d):
+        arrived(hx.at[ys[d]], h_recv.at[0, d])
+        hs[ys[d]] = (part[ys[d], kept, :].astype(F32) + hx[ys[d]].astype(F32)).astype(BF16)
+
+    low, high = pl.ds(0, HP), pl.ds(HP, HP)
+
+    def y_far(c):
+        remote(mine(c, FAR).at[low], tab.at[c, 0], y_sent, y_recv.at[c, 0], dev_yn).start()
+        remote(mine(c, FAR).at[high], tab.at[c, 1], y_sent, y_recv.at[c, 0], dev_yp).start()
+
+    def y_next_half(c):
+        remote(mine(c, NEXT).at[high], r12.at[c, 0, high], y_sent, y_recv.at[c, 1], dev_yn).start()
+
+    def y_prev_half(c):
+        remote(mine(c, PREV).at[low], r12.at[c, 1, low], y_sent, y_recv.at[c, 1], dev_yp).start()
+
+    def y_second(c):
+        arrived(tab.at[c], y_recv.at[c, 0])
+        sab[c, 0] = (tab[c, 0].astype(F32) + mine(c, NEXT)[low, :].astype(F32)).astype(BF16)
+        remote(sab.at[c, 0], r12.at[c, 0, low], y_sent, y_recv.at[c, 1], dev_yn).start()
+        sab[c, 1] = (tab[c, 1].astype(F32) + mine(c, PREV)[high, :].astype(F32)).astype(BF16)
+        remote(sab.at[c, 1], r12.at[c, 1, high], y_sent, y_recv.at[c, 1], dev_yp).start()
+
+    def y_total(c):
+        arrived(r12.at[c], y_recv.at[c, 1])
+        return (mine(c, OWN)[...].astype(F32) + r12[c, 0].astype(F32) + r12[c, 1].astype(F32)).astype(BF16)
+
+    def x_swap(c):
+        xs[c] = y_total(c)
+        remote(xs.at[c], xr.at[c], y_sent, y_recv.at[c, 2], dev_x).start()
+
+    def group_far(g):
+        project(g, FAR)
         for c in chunks(g):
-            remote(part.at[ys[FAR], half(c, 0)], tab.at[c, 0], y_sent, y_recv.at[c, 0], dev_yn).start()
-            remote(part.at[ys[FAR], half(c, 1)], tab.at[c, 1], y_sent, y_recv.at[c, 0], dev_yp).start()
-
-    def y_near(g):
+            y_far(c)
+
+    def group_near(g):
         project(g, NEXT)
         for c in chunks(g):
-            remote(
-                part.at[ys[NEXT], half(c, 1)], r12.at[c, 0, pl.ds(HP, HP)], y_sent, y_recv.at[c, 1], dev_yn
-            ).start()
+            y_next_half(c)
         project(g, PREV)
         for c in chunks(g):
-            remote(
-                part.at[ys[PREV], half(c, 0)], r12.at[c, 1, pl.ds(0, HP)], y_sent, y_recv.at[c, 1], dev_yp
-            ).start()
-
-    def y_second(g):
+            y_prev_half(c)
+
+    def group_second(g):
         for c in chunks(g):
-            arrived(tab.at[c], y_recv.at[c, 0])
-            sab[c, 0] = (tab[c, 0].astype(F32) + part[ys[NEXT], half(c, 0), :].astype(F32)).astype(BF16)
-            remote(sab.at[c, 0], r12.at[c, 0, pl.ds(0, HP)], y_sent, y_recv.at[c, 1], dev_yn).start()
-            sab[c, 1] = (tab[c, 1].astype(F32) + part[ys[PREV], half(c, 1), :].astype(F32)).astype(BF16)
-            remote(sab.at[c, 1], r12.at[c, 1, pl.ds(HP, HP)], y_sent, y_recv.at[c, 1], dev_yp).start()
-
-    def x_swap(c):
-        arrived(r12.at[c], y_recv.at[c, 1])
-        xs[c] = (
-            part[ys[OWN], chunk(c), :].astype(F32) + r12[c, 0].astype(F32) + r12[c, 1].astype(F32)
-        ).astype(BF16)
-        remote(xs.at[c], xr.at[c], y_sent, y_recv.at[c, 2], dev_x).start()
+            y_second(c)
+
+    def group_swap(g):
+        for c in chunks(g):
+            x_swap(c)
+
+    def first_far():
+        x_take(FAR)
+        y_far(0)
+
+    def first_near():
+        x_take(NEXT)
+        y_next_half(0)
+        x_take(PREV)
+        y_prev_half(0)
+
+    def x_share(d):
+        piece = cf.at[ys[d], kept]
+        remote(piece, piece, y_sent, h_recv.at[1, d], dev_x).start()
+
+    def x_shared(d):
+        arrived(cf.at[ys[d], given], h_recv.at[1, d])
+        to_core(0, d)
+
+    def first_third():
+        x_take(OWN)
+        cf[ys[OWN], kept, :] = y_total(0)
+        piece = cf.at[ys[OWN], kept]
+        remote(piece, piece, y_sent, g_recv.at[0, 0], dev_yn).start()
+        remote(piece, piece, y_sent, g_recv.at[0, 1], dev_yp).start()
+        x_share(OWN)
+
+    def kept_half(h):
+        return pl.ds(pl.multiple_of(x_lo * CP + h * HP, HP), HP)
+
+    def first_fourth():
+        arrived(cf.at[ys[PREV], kept], g_recv.at[0, 0])
+        piece = cf.at[ys[PREV], kept_half(0)]
+        remote(piece, piece, y_sent, g_recv.at[0, 2], dev_yn).start()
+        x_share(PREV)
+        arrived(cf.at[ys[NEXT], kept], g_recv.at[0, 1])
+        piece = cf.at[ys[NEXT], kept_half(1)]
+        remote(piece, piece, y_sent, g_recv.at[0, 2], dev_yp).start()
+        x_share(NEXT)
+
+    def first_last():
+        arrived(cf.at[ys[FAR], kept], g_recv.at[0, 2])
+        x_share(FAR)
 
     def to_core(g, d):
         sem = c_recv.at[g] if d == OWN else c_recv.at[NG + d - 1]
@@ -174,9 +254,9 @@
             return jnp.where(emp_ref[...] == e, ee_ref[e], value)
 
         zero = jnp.zeros((8, 128), F32)
-        low = lax.fori_loop(0, 64, occupied, zero, unroll=8)
-        high = lax.fori_loop(0, 256, empty, zero, unroll=8)
-        gaps[0] = high - low
+        below = lax.fori_loop(0, 64, occupied, zero, unroll=8)
+        above = lax.fori_loop(0, 256, empty, zero, unroll=8)
+        gaps[0] = above - below
 
     def send_gaps():
         remote(gaps.at[0], gaps.at[1], gap_sent, c_recv.at[NG + 3], dev_core).start()
@@ -242,6 +322,9 @@
             zs[slot[d], q, 1] = (val[d, q, there, cols(z_prev)] + zt[slot[d], q, 1].astype(F32)).astype(BF16)
             remote(zs.at[slot[d], q, 1], zr.at[slot[d], q, 1], c_sent, z_recv.at[d, q], dev_zp).start()
 
+    ours = pl.ds(pl.multiple_of(core * 64, 64), 64)
+    theirs = pl.ds(pl.multiple_of((1 - core) * 64, 64), 64)
+
     def z_third(d, q):
         @pl.when(root[d])
         def _():
@@ -252,93 +335,93 @@
                     val[d, q, rows, cols(z)]
                     + zr[slot[d], q, first].astype(F32)
                     + zr[slot[d], q, second].astype(F32)
-                )
+                ).T
 
             @pl.when(slot[d] == x_hi)
             def _():
-                zacc[q, 0] = total(here, 0, 3)
-                zacc[q, 1] = total(there, 2, 1)
+                fin[2 * q] = total(here, 0, 3)
+                fin[2 * q + 1] = total(there, 2, 1)
+                remote(
+                    fin.at[pl.ds(2 * q, 2), theirs, :], finr.at[pl.ds(2 * q, 2)], c_sent, x_recv.at[q, 2], dev_core
+                ).start()
 
             @pl.when(slot[d] != x_hi)
             def _():
                 zxs[q, 0] = total(here, 0, 3).astype(BF16)
                 zxs[q, 1] = total(there, 2, 1).astype(BF16)
-                remote(zxs.at[q], zxr.at[q], c_sent, x_recv.at[q, 0], dev_xh).start()
+                remote(zxs.at[q, :, ours, :], zxr.at[q, 0], c_sent, x_recv.at[q, 0], dev_xh).start()
+                remote(zxs.at[q, :, theirs, :], zxr.at[q, 1], c_sent, x_recv.at[q, 1], dev_xhc).start()
 
     def finish(q):
-        arrived(zxr.at[q], x_recv.at[q, 0])
-        for h in range(2):
-            fin[2 * q + h] = (zacc[q, h] + zxr[q, h].astype(F32)).T
-        theirs = pl.ds(pl.multiple_of((1 - core) * 64, 64), 64)
-        remote(
-            fin.at[pl.ds(2 * q, 2), theirs, :], finr.at[pl.ds(2 * q, 2)], c_sent, x_recv.at[q, 1], dev_core
-        ).start()
-        mine = pl.ds(pl.multiple_of(core * 64, 64), 64)
-        out_ref[pl.ds(core * NW + 2 * q, 2)] = fin[pl.ds(2 * q, 2), mine, :]
-
-    def take(q):
-        arrived(finr.at[pl.ds(2 * q, 2)], x_recv.at[q, 1])
-        out_ref[pl.ds((1 - core) * NW + 2 * q, 2)] = finr[pl.ds(2 * q, 2)]
-
-    project(0, FAR)
+        arrived(zxr.at[q, 0], x_recv.at[q, 0])
+        out_ref[pl.ds(core * NW + 2 * q, 2)] = fin[pl.ds(2 * q, 2), ours, :] + zxr[q, 0].astype(F32)
+        arrived(finr.at[pl.ds(2 * q, 2)], x_recv.at[q, 2])
+        arrived(zxr.at[q, 1], x_recv.at[q, 1])
+        out_ref[pl.ds((1 - core) * NW + 2 * q, 2)] = finr[pl.ds(2 * q, 2)] + zxr[q, 1].astype(F32)
+
+    project(1, FAR)
     pl.semaphore_wait(barrier, len(peers))
-    y_far(0)
-    project(1, FAR)
-    y_far(1)
-    y_near(0)
+    y_far(2)
+    y_far(3)
+    x_give(FAR)
+    group_far(2)
+    group_near(1)
+    x_give(NEXT)
+    group_second(1)
+    x_give(PREV)
+    group_far(3)
+    first_far()
+    group_near(2)
+    group_second(2)
+    project(1, OWN)
+    first_near()
+    group_swap(1)
+    x_give(OWN)
+    group_near(3)
     y_second(0)
-    project(2, FAR)
-    y_far(2)
-    y_near(1)
-    y_second(1)
-    project(3, FAR)
-    y_far(3)
-    y_near(2)
-    project(0, OWN)
-    x_swap(0)
-    x_swap(1)
-    y_second(2)
-    y_near(3)
-    project(1, OWN)
-    x_swap(2)
-    x_swap(3)
+    group_second(3)
     project(2, OWN)
-    y_second(3)
-    y_third(0)
-    project(3, OWN)
     find_gaps()
     send_gaps()
-    x_swap(4)
-    x_swap(5)
+    group_swap(2)
+    project(3, OWN)
+    first_third()
     y_third(1)
+    group_swap(3)
     find_factors()
-    weigh(0)
-    x_swap(6)
-    x_swap(7)
     y_third(2)
+    x_shared(OWN)
     weigh(1)
+    first_fourth()
     y_third(3)
     weigh(2)
+    weigh(0)
+    y_fourth(1)
     weigh(3)
-    y_fourth(0)
-    y_fourth(1)
-    for q in range(NQ):
-        tiles(OWN, q)
+    tiles(OWN, 0)
     y_fourth(2)
+    tiles(OWN, 1)
+    tiles(OWN, 2)
+    z_second(OWN, 0)
+    tiles(OWN, 3)
+    x_shared(PREV)
+    x_shared(NEXT)
     y_fourth(3)
+    first_last()
+    for q in range(1, NQ):
+        z_second(OWN, q)
     from_core(NEXT)
     for q in range(NQ):
-        z_second(OWN, q)
         tiles(NEXT, q)
+    x_shared(FAR)
+    y_last(1)
     from_core(PREV)
-    y_last(0)
-    y_last(1)
-    for q in range(NQ):
+    for q in range(NQ):
+        tiles(PREV, q)
         z_third(OWN, q)
         z_second(NEXT, q)
-        tiles(PREV, q)
-    y_last(2)
-    y_last(3)
+        if q < 2:
+            y_last(q + 2)
     from_core(FAR)
     for q in range(NQ):
         z_second(PREV, q)
@@ -352,8 +435,6 @@
         z_third(FAR, q)
     for q in range(NQ):
         finish(q)
-    for q in range(NQ):
-        take(q)
     arrived(pw.at[pl.ds(0, 896)], y_sent)
     arrived(pw, c_sent)
     arrived(gaps.at[0], gap_sent)
@@ -362,7 +443,7 @@
 def on_device(pair_waves, subspace_basis, occ_band, empty_band, occ_energy, empty_energy, freq_grid, freq_index):
     vmem = pl.BlockSpec(memory_space=pltpu.VMEM)
     smem = pl.BlockSpec(memory_space=pltpu.SMEM)
-    hbm = pl.BlockSpec(memory_space=pl.ANY)
+    hbm = pl.BlockSpec(memory_space=pltpu.HBM)
     dma = pltpu.SemaphoreType.DMA
     out = pl.pallas_call(
         kernel,
@@ -377,6 +458,8 @@
             pltpu.VMEM((NW * ROWS, 2 * PL), BF16),
             pltpu.VMEM((2, 8, 128), F32),
             pltpu.VMEM((2, NW, 8, 128), F32),
+            pltpu.VMEM((4, CP, BC), BF16),
+            pltpu.VMEM((4, CP, BC), BF16),
             pltpu.VMEM((NC, 2, HP, BC), BF16),
             pltpu.VMEM((NC, 2, HP, BC), BF16),
             pltpu.VMEM((NC, 2, CP, BC), BF16),
@@ -388,23 +471,28 @@
             pltpu.VMEM((2, NQ, 2, ROWS, ROWS), BF16),
             pltpu.VMEM((2, NQ, 4, ROWS, ROWS), BF16),
             pltpu.VMEM((NQ, 2, ROWS, ROWS), BF16),
-            pltpu.VMEM((NQ, 2, ROWS, ROWS), BF16),
-            pltpu.VMEM((NQ, 2, ROWS, ROWS), F32),
+            pltpu.VMEM((NQ, 2, 2, 64, ROWS), BF16),
             pltpu.VMEM((NW, ROWS, ROWS), F32),
             pltpu.VMEM((NW, 64, ROWS), F32),
             dma((NG + 4,)),
             dma((3,)),
             dma((NC, 3)),
             dma((NG, 3)),
+            dma((2, 4)),
             dma((4, NQ)),
-            dma((NQ, 2)),
+            dma((NQ, 3)),
             dma((NG + 4,)),
         ],
-        compiler_params=pltpu.CompilerParams(collective_id=0, has_side_effects=True),
+        compiler_params=pltpu.CompilerParams(collective_id=0, has_side_effects=True, vmem_limit_bytes=48 << 20),
         cost_estimate=pl.CostEstimate(flops=9 << 30, bytes_accessed=9 << 20, transcendentals=0),
     )(
-        occ_band.reshape(8, 128), empty_band.reshape(8, 128), pair_waves, subspace_basis,
-        occ_energy, empty_energy, freq_grid, freq_index,
+        *(
+            pltpu.with_memory_space_constraint(array, pltpu.HBM)
+            for array in (
+                occ_band.reshape(8, 128), empty_band.reshape(8, 128), pair_waves, subspace_basis,
+                occ_energy, empty_energy, freq_grid, freq_index,
+            )
+        )
     )
     return jnp.swapaxes(out, 1, 2)
 

time: 71.3 us -> 63.8 us (0.89)
  Pallas kernels: 69.2 us -> 62.3 us
  local copies, waits for them, and re-layouts: 1.89 us -> 0.8 us
    pallas_call x1, Pallas kernels: 69.2 us -> 62.3 us  [on_device(): pl.pallas_call(kernel, out_shape=jax.ShapeDtypeStruct((NFREQ, 64, ROWS),...]
    unnamed x1, local copies, waits for them, and re-layouts: 1.89 us -> 0.8 us
where the time goes in v3:
time: 63.8 us; the launch traced here: 63.1 us
  Pallas kernels  62.3 us (98%)
  local copies, waits for them, and re-layouts  0.8 us (1%)
    pallas_call x1, Pallas kernels, on_device(): pl.pallas_call(kernel, out_shape=jax.ShapeDtypeStruct((NFREQ, 64, ROWS),...  62.3 us

profile of v3, /device:TPU:33, one launch (start us, length us, event | category | flops | bytes accessed | tf_op | source)
XLA Modules:
  0.0 63.1 jit_solution(17553783879438572332)
XLA Ops:
  0.0 62.3 %shard_map.82 = f32[16,64,128]{2,1,0:T(8,128)S(1)} custom-call(s32[8,128]{1,0:T(8,128)} %bitcast.4, s32[8,128]{1,0:T(8,128)} %bitcast.5, bf16[1024,2048]{1,0:T(8,128)(2,1)} %pw_hbm.1, bf16[2048,1024]{1,0:T(8,128)(2,1)} %basis_hbm.1, f32[64]{0:T(128)} %oe_ref.1, f32[256]{0:T(256)} %ee_ref.1, f32[16]{0:T(128)} %fg_ref.1, s32[16]{0:T(128)} %fi_ref.1), custom_call_target="tpu_custom_call" | custom-call | flops 9663676416 | bytes 9437184 | tf_op jit(solution)/shard_map/pallas_call | solution.py:448
  62.3 0.8 %copy.10 = f32[16,128,64]{1,2,0:T(8,128)} copy(f32[16,128,64]{1,2,0:T(8,128)S(1)} %bitcast.3) | data formatting | bytes 1048576

commit v4 on v3

--- a/solution.py
+++ b/solution.py
@@ -29,11 +29,12 @@
 
 
 def kernel(
-    occ_ref, emp_ref, pw_hbm, basis_hbm, oe_ref, ee_ref, fg_ref, fi_ref, out_ref,
+    occ_hbm, emp_hbm, pw_hbm, basis_hbm, oe_hbm, ee_hbm, fg_hbm, fi_hbm, out_ref,
+    occ_ref, emp_ref, oe_ref, ee_ref, fg_ref, fi_ref,
     pw, basis, part, cf, wt, gaps, fac,
     hx, hs, tab, sab, r12, xs, xr,
     val, zo, zs, zt, zr, zxs, zxr, fin, finr,
-    load_sem, send_sem, y_recv, g_recv, h_recv, z_recv, x_recv, c_recv,
+    load_sem, small_sem, send_sem, y_recv, g_recv, h_recv, z_recv, x_recv, c_recv,
 ):
     me_pw, me_pair = lax.axis_index("pw"), lax.axis_index("pair")
     x_lo, y = me_pw // 4, me_pw % 4
@@ -84,6 +85,17 @@
     pw_loads[2].start()
     pw_loads[3].start()
     load_basis(OWN)
+    small_loads = [
+        pltpu.make_async_copy(src, dst, small_sem.at[k])
+        for k, (src, dst) in enumerate(
+            (
+                (occ_hbm, occ_ref), (emp_hbm, emp_ref), (oe_hbm, oe_ref),
+                (ee_hbm, ee_ref), (fg_hbm, fg_ref), (fi_hbm, fi_ref),
+            )
+        )
+    ]
+    for load in small_loads:
+        load.start()
 
     barrier = pltpu.get_barrier_semaphore()
     for peer in peers:
@@ -202,15 +214,17 @@
     def kept_half(h):
         return pl.ds(pl.multiple_of(x_lo * CP + h * HP, HP), HP)
 
-    def first_fourth():
+    def first_take():
         arrived(cf.at[ys[PREV], kept], g_recv.at[0, 0])
+        x_share(PREV)
+        arrived(cf.at[ys[NEXT], kept], g_recv.at[0, 1])
+        x_share(NEXT)
+
+    def first_forward():
         piece = cf.at[ys[PREV], kept_half(0)]
         remote(piece, piece, y_sent, g_recv.at[0, 2], dev_yn).start()
-        x_share(PREV)
-        arrived(cf.at[ys[NEXT], kept], g_recv.at[0, 1])
         piece = cf.at[ys[NEXT], kept_half(1)]
         remote(piece, piece, y_sent, g_recv.at[0, 2], dev_yp).start()
-        x_share(NEXT)
 
     def first_last():
         arrived(cf.at[ys[FAR], kept], g_recv.at[0, 2])
@@ -227,26 +241,31 @@
         for c in chunks(g):
             arrived(xr.at[c], y_recv.at[c, 2])
             cf[ys[OWN], chunk(c), :] = (xs[c].astype(F32) + xr[c].astype(F32)).astype(BF16)
-        piece = cf.at[ys[OWN], group(g)]
-        remote(piece, piece, y_sent, g_recv.at[g, 0], dev_yn).start()
-        remote(piece, piece, y_sent, g_recv.at[g, 1], dev_yp).start()
+            piece = cf.at[ys[OWN], chunk(c)]
+            remote(piece, piece, y_sent, g_recv.at[g, 0], dev_yn).start()
+            remote(piece, piece, y_sent, g_recv.at[g, 1], dev_yp).start()
         to_core(g, OWN)
 
-    def y_fourth(g):
+    def y_take(g):
         arrived(cf.at[ys[PREV], group(g)], g_recv.at[g, 0])
+        to_core(g, PREV)
+        arrived(cf.at[ys[NEXT], group(g)], g_recv.at[g, 1])
+        to_core(g, NEXT)
+
+    def y_forward(g):
         piece = cf.at[ys[PREV], group_half(g, 0)]
         remote(piece, piece, y_sent, g_recv.at[g, 2], dev_yn).start()
-        arrived(cf.at[ys[NEXT], group(g)], g_recv.at[g, 1])
         piece = cf.at[ys[NEXT], group_half(g, 1)]
         remote(piece, piece, y_sent, g_recv.at[g, 2], dev_yp).start()
-        to_core(g, PREV)
-        to_core(g, NEXT)
 
     def y_last(g):
         arrived(cf.at[ys[FAR], group(g)], g_recv.at[g, 2])
         to_core(g, FAR)
 
     def find_gaps():
+        for load in small_loads:
+            load.wait()
+
         def occupied(e, value):
             return jnp.where(occ_ref[...] == e, oe_ref[e], value)
 
@@ -272,22 +291,22 @@
                     below / (below * below + broadening_sq) - above / (above * above + broadening_sq)
                 )
 
-    def weigh(g):
-        arrived(cf.at[ys[OWN], pl.ds(PL + g * GP, GP)], c_recv.at[g])
+    def weigh(g, src):
+        if src:
+            arrived(cf.at[ys[OWN], pl.ds(PL + g * GP, GP)], c_recv.at[g])
         rows = pl.ds(pl.multiple_of(x_lo * ROWS, ROWS), ROWS)
-        for src in range(2):
-            for r in range(GP // 128):
-                first = src * PL + g * GP + r * 128
-                block = cf[ys[OWN], pl.ds(first, 128), rows].astype(F32).T
-
-                def one(n, carry):
-                    row = fac[src, n, pl.ds(g * (GP // 128) + r, 1), :]
-                    wt[pl.ds(pl.multiple_of(n * ROWS, ROWS), ROWS), pl.ds(first, 128)] = (
-                        block * row
-                    ).astype(BF16)
-                    return carry
-
-                lax.fori_loop(0, NW, one, 0, unroll=2)
+        for r in range(GP // 128):
+            first = src * PL + g * GP + r * 128
+            block = cf[ys[OWN], pl.ds(first, 128), rows].astype(F32).T
+
+            def one(n, carry):
+                row = fac[src, n, pl.ds(g * (GP // 128) + r, 1), :]
+                wt[pl.ds(pl.multiple_of(n * ROWS, ROWS), ROWS), pl.ds(first, 128)] = (
+                    block * row
+                ).astype(BF16)
+                return carry
+
+            lax.fori_loop(0, NW, one, 0, unroll=2)
 
     slot = [ys[d] % 2 for d in range(4)]
     root = [(z % 2) == ys[d] // 2 for d in range(4)]
@@ -390,38 +409,55 @@
     group_swap(3)
     find_factors()
     y_third(2)
+    weigh(1, 0)
     x_shared(OWN)
-    weigh(1)
-    first_fourth()
+    weigh(1, 1)
+    weigh(2, 0)
+    weigh(0, 0)
+    weigh(2, 1)
     y_third(3)
-    weigh(2)
-    weigh(0)
-    y_fourth(1)
-    weigh(3)
+    weigh(3, 0)
+    weigh(0, 1)
+    first_take()
+    first_forward()
+    weigh(3, 1)
     tiles(OWN, 0)
-    y_fourth(2)
     tiles(OWN, 1)
+    y_take(1)
     tiles(OWN, 2)
-    z_second(OWN, 0)
     tiles(OWN, 3)
     x_shared(PREV)
     x_shared(NEXT)
-    y_fourth(3)
-    first_last()
-    for q in range(1, NQ):
-        z_second(OWN, q)
+    y_take(2)
+    y_forward(1)
+    y_take(3)
+    y_forward(2)
+    y_forward(3)
+    z_second(OWN, 0)
+    z_second(OWN, 1)
     from_core(NEXT)
     for q in range(NQ):
         tiles(NEXT, q)
+        if q < 2:
+            z_second(OWN, q + 2)
+    from_core(PREV)
+    first_last()
+    tiles(PREV, 0)
+    z_third(OWN, 0)
+    z_second(NEXT, 0)
+    y_last(1)
+    tiles(PREV, 1)
+    z_third(OWN, 1)
+    z_second(NEXT, 1)
+    y_last(2)
+    tiles(PREV, 2)
+    z_third(OWN, 2)
+    z_second(NEXT, 2)
     x_shared(FAR)
-    y_last(1)
-    from_core(PREV)
-    for q in range(NQ):
-        tiles(PREV, q)
-        z_third(OWN, q)
-        z_second(NEXT, q)
-        if q < 2:
-            y_last(q + 2)
+    y_last(3)
+    tiles(PREV, 3)
+    z_third(OWN, 3)
+    z_second(NEXT, 3)
     from_core(FAR)
     for q in range(NQ):
         z_second(PREV, q)
@@ -442,15 +478,20 @@
 
 def on_device(pair_waves, subspace_basis, occ_band, empty_band, occ_energy, empty_energy, freq_grid, freq_index):
     vmem = pl.BlockSpec(memory_space=pltpu.VMEM)
-    smem = pl.BlockSpec(memory_space=pltpu.SMEM)
     hbm = pl.BlockSpec(memory_space=pltpu.HBM)
     dma = pltpu.SemaphoreType.DMA
     out = pl.pallas_call(
         kernel,
         out_shape=jax.ShapeDtypeStruct((NFREQ, 64, ROWS), F32),
-        in_specs=[vmem, vmem, hbm, hbm, smem, smem, smem, smem],
+        in_specs=[hbm] * 8,
         out_specs=vmem,
         scratch_shapes=[
+            pltpu.VMEM((8, 128), jnp.int32),
+            pltpu.VMEM((8, 128), jnp.int32),
+            pltpu.SMEM((64,), F32),
+            pltpu.SMEM((256,), F32),
+            pltpu.SMEM((NFREQ,), F32),
+            pltpu.SMEM((NFREQ,), jnp.int32),
             pltpu.VMEM((PL, PWL), BF16),
             pltpu.VMEM((4, PWL, BC), BF16),
             pltpu.VMEM((4, PL, BC), BF16),
@@ -475,6 +516,7 @@
             pltpu.VMEM((NW, ROWS, ROWS), F32),
             pltpu.VMEM((NW, 64, ROWS), F32),
             dma((NG + 4,)),
+            dma((6,)),
             dma((3,)),
             dma((NC, 3)),
             dma((NG, 3)),

time: 63.8 us -> 61.8 us (0.969)
  Pallas kernels: 62.3 us -> 60.9 us
    pallas_call x1, Pallas kernels: 62.3 us -> 60.9 us  [on_device(): pl.pallas_call(kernel, out_shape=jax.ShapeDtypeStruct((NFREQ, 64, ROWS),...]
where the time goes in v4:
time: 61.8 us; the launch traced here: 61.7 us
  Pallas kernels  60.9 us (99%)
  local copies, waits for them, and re-layouts  0.8 us (1%)
    pallas_call x1, Pallas kernels, on_device(): pl.pallas_call(kernel, out_shape=jax.ShapeDtypeStruct((NFREQ, 64, ROWS),...  60.9 us

profile of v4, /device:TPU:33, one launch (start us, length us, event | category | flops | bytes accessed | tf_op | source)
XLA Modules:
  0.0 61.7 jit_solution(9786489176583585148)
XLA Ops:
  0.0 60.9 %shard_map.82 = f32[16,64,128]{2,1,0:T(8,128)S(1)} custom-call(s32[8,128]{1,0:T(8,128)} %bitcast.4, s32[8,128]{1,0:T(8,128)} %bitcast.5, bf16[1024,2048]{1,0:T(8,128)(2,1)} %pw_hbm.1, bf16[2048,1024]{1,0:T(8,128)(2,1)} %basis_hbm.1, f32[64]{0:T(128)} %oe_hbm.1, f32[256]{0:T(256)} %ee_hbm.1, f32[16]{0:T(128)} %fg_hbm.1, s32[16]{0:T(128)} %fi_hbm.1), custom_call_target="tpu_custom_call" | custom-call | flops 9663676416 | bytes 9437184 | tf_op jit(solution)/shard_map/pallas_call | solution.py:483
  60.9 0.8 %copy.10 = f32[16,128,64]{1,2,0:T(8,128)} copy(f32[16,128,64]{1,2,0:T(8,128)S(1)} %bitcast.3) | data formatting | bytes 1048576

commit v5 on v4

--- a/solution.py
+++ b/solution.py
@@ -26,6 +26,7 @@
 NQ = 4
 QR = NW * ROWS // NQ
 OWN, NEXT, FAR, PREV = range(4)
+SECOND, THIRD = NEXT, PREV
 
 
 def kernel(
@@ -234,9 +235,6 @@
         sem = c_recv.at[g] if d == OWN else c_recv.at[NG + d - 1]
         remote(cf.at[ys[d], group(g)], cf.at[ys[d], pl.ds(PL + g * GP, GP)], c_sent, sem, dev_core).start()
 
-    def from_core(d):
-        arrived(cf.at[ys[d], pl.ds(PL, PL)], c_recv.at[NG + d - 1])
-
     def y_third(g):
         for c in chunks(g):
             arrived(xr.at[c], y_recv.at[c, 2])
@@ -308,15 +306,21 @@
 
             lax.fori_loop(0, NW, one, 0, unroll=2)
 
-    slot = [ys[d] % 2 for d in range(4)]
-    root = [(z % 2) == ys[d] // 2 for d in range(4)]
+    turn = [OWN, 3 - 2 * (y % 2), FAR, 1 + 2 * (y % 2)]
+    yt = [ys[OWN], (y + 3 - 2 * (y % 2)) % 4, ys[FAR], (y + 1 + 2 * (y % 2)) % 4]
+    slot = [yt[d] % 2 for d in range(4)]
+    root = [(z % 2) == yt[d] // 2 for d in range(4)]
+
+    def whole(d):
+        arrived(cf.at[yt[d], pl.ds(PL, PL)], c_recv.at[NG + turn[d] - 1])
+
     here, there = pl.ds(0, ROWS), pl.ds(ROWS, ROWS)
 
     def cols(t):
         return pl.ds(pl.multiple_of((t // 2) * 128, 128), 128)
 
     def tiles(d, q):
-        val[d, q] = jnp.dot(wt[pl.ds(q * QR, QR), :], cf[ys[d]], preferred_element_type=F32)
+        val[d, q] = jnp.dot(wt[pl.ds(q * QR, QR), :], cf[yt[d]], preferred_element_type=F32)
 
         @pl.when(root[d])
         def _():
@@ -402,10 +406,10 @@
     project(2, OWN)
     find_gaps()
     send_gaps()
+    y_third(1)
     group_swap(2)
     project(3, OWN)
     first_third()
-    y_third(1)
     group_swap(3)
     find_factors()
     y_third(2)
@@ -435,38 +439,46 @@
     y_forward(3)
     z_second(OWN, 0)
     z_second(OWN, 1)
-    from_core(NEXT)
-    for q in range(NQ):
-        tiles(NEXT, q)
-        if q < 2:
-            z_second(OWN, q + 2)
-    from_core(PREV)
+    whole(SECOND)
+    tiles(SECOND, 0)
+    z_second(OWN, 2)
+    tiles(SECOND, 1)
+    z_second(OWN, 3)
+    tiles(SECOND, 2)
+    tiles(SECOND, 3)
     first_last()
-    tiles(PREV, 0)
+    whole(THIRD)
+    tiles(THIRD, 0)
+    y_last(1)
+    z_second(SECOND, 0)
+    tiles(THIRD, 1)
+    z_second(SECOND, 1)
+    y_last(2)
+    tiles(THIRD, 2)
+    y_last(3)
+    tiles(THIRD, 3)
+    x_shared(FAR)
+    z_second(SECOND, 2)
+    z_second(SECOND, 3)
     z_third(OWN, 0)
-    z_second(NEXT, 0)
-    y_last(1)
-    tiles(PREV, 1)
     z_third(OWN, 1)
-    z_second(NEXT, 1)
-    y_last(2)
-    tiles(PREV, 2)
-    z_third(OWN, 2)
-    z_second(NEXT, 2)
-    x_shared(FAR)
-    y_last(3)
-    tiles(PREV, 3)
-    z_third(OWN, 3)
-    z_second(NEXT, 3)
-    from_core(FAR)
-    for q in range(NQ):
-        z_second(PREV, q)
-        tiles(FAR, q)
-    for q in range(NQ):
-        z_third(NEXT, q)
+    z_second(THIRD, 0)
+    whole(FAR)
+    tiles(FAR, 0)
+    tiles(FAR, 1)
+    z_second(THIRD, 1)
+    tiles(FAR, 2)
+    tiles(FAR, 3)
+    z_second(THIRD, 2)
+    z_second(THIRD, 3)
     for q in range(NQ):
         z_second(FAR, q)
-        z_third(PREV, q)
+    z_third(OWN, 2)
+    z_third(OWN, 3)
+    for q in range(NQ):
+        z_third(SECOND, q)
+    for q in range(NQ):
+        z_third(THIRD, q)
     for q in range(NQ):
         z_third(FAR, q)
     for q in range(NQ):

time: 61.8 us -> 59.4 us (0.961)
  Pallas kernels: 60.9 us -> 58.5 us
    pallas_call x1, Pallas kernels: 60.9 us -> 58.5 us  [on_device(): pl.pallas_call(kernel, out_shape=jax.ShapeDtypeStruct((NFREQ, 64, ROWS),...]
where the time goes in v5:
time: 59.4 us; the launch traced here: 59.3 us
  Pallas kernels  58.5 us (98%)
  local copies, waits for them, and re-layouts  0.8 us (1%)
    pallas_call x1, Pallas kernels, on_device(): pl.pallas_call(kernel, out_shape=jax.ShapeDtypeStruct((NFREQ, 64, ROWS),...  58.5 us

profile of v5, /device:TPU:33, one launch (start us, length us, event | category | flops | bytes accessed | tf_op | source)
XLA Modules:
  0.0 59.3 jit_solution(4166153335847025521)
XLA Ops:
  0.0 58.5 %shard_map.82 = f32[16,64,128]{2,1,0:T(8,128)S(1)} custom-call(s32[8,128]{1,0:T(8,128)} %bitcast.4, s32[8,128]{1,0:T(8,128)} %bitcast.5, bf16[1024,2048]{1,0:T(8,128)(2,1)} %pw_hbm.1, bf16[2048,1024]{1,0:T(8,128)(2,1)} %basis_hbm.1, f32[64]{0:T(128)} %oe_hbm.1, f32[256]{0:T(256)} %ee_hbm.1, f32[16]{0:T(128)} %fg_hbm.1, s32[16]{0:T(128)} %fi_hbm.1), custom_call_target="tpu_custom_call" | custom-call | flops 9663676416 | bytes 9437184 | tf_op jit(solution)/shard_map/pallas_call | solution.py:495
  58.5 0.8 %copy.10 = f32[16,128,64]{1,2,0:T(8,128)} copy(f32[16,128,64]{1,2,0:T(8,128)S(1)} %bitcast.3) | data formatting | bytes 1048576

commit v6 on v5

--- a/solution.py
+++ b/solution.py
@@ -121,6 +121,15 @@
             pw[group(g), :], basis[ys[d]], preferred_element_type=F32
         ).astype(BF16)
 
+    def first_loads():
+        pw_loads[1].wait()
+        arrived(basis.at[ys[FAR]], load_sem.at[NG + FAR])
+
+    def project_chunk(c):
+        part[ys[FAR], chunk(c), :] = jnp.dot(
+            pw[chunk(c), :], basis[ys[FAR]], preferred_element_type=F32
+        ).astype(BF16)
+
     def chunks(g):
         return range(g * GC, (g + 1) * GC)
 
@@ -242,7 +251,8 @@
             piece = cf.at[ys[OWN], chunk(c)]
             remote(piece, piece, y_sent, g_recv.at[g, 0], dev_yn).start()
             remote(piece, piece, y_sent, g_recv.at[g, 1], dev_yp).start()
-        to_core(g, OWN)
+            there_too = cf.at[ys[OWN], pl.ds(PL + c * CP, CP)]
+            remote(piece, there_too, c_sent, c_recv.at[g], dev_core).start()
 
     def y_take(g):
         arrived(cf.at[ys[PREV], group(g)], g_recv.at[g, 0])
@@ -382,9 +392,11 @@
         arrived(zxr.at[q, 1], x_recv.at[q, 1])
         out_ref[pl.ds((1 - core) * NW + 2 * q, 2)] = finr[pl.ds(2 * q, 2)] + zxr[q, 1].astype(F32)
 
-    project(1, FAR)
+    first_loads()
+    project_chunk(2)
     pl.semaphore_wait(barrier, len(peers))
     y_far(2)
+    project_chunk(3)
     y_far(3)
     x_give(FAR)
     group_far(2)
@@ -400,8 +412,8 @@
     first_near()
     group_swap(1)
     x_give(OWN)
+    y_second(0)
     group_near(3)
-    y_second(0)
     group_second(3)
     project(2, OWN)
     find_gaps()
@@ -462,15 +474,11 @@
     z_second(SECOND, 3)
     z_third(OWN, 0)
     z_third(OWN, 1)
-    z_second(THIRD, 0)
     whole(FAR)
-    tiles(FAR, 0)
-    tiles(FAR, 1)
-    z_second(THIRD, 1)
-    tiles(FAR, 2)
-    tiles(FAR, 3)
-    z_second(THIRD, 2)
-    z_second(THIRD, 3)
+    for q in range(NQ):
+        tiles(FAR, q)
+    for q in range(NQ):
+        z_second(THIRD, q)
     for q in range(NQ):
         z_second(FAR, q)
     z_third(OWN, 2)

time: 59.4 us -> 59 us (level)
  no operation moved by 1% of the time
where the time goes in v6:
time: 59 us; the launch traced here: 58.9 us
  Pallas kernels  58.1 us (98%)
  local copies, waits for them, and re-layouts  0.8 us (1%)
    pallas_call x1, Pallas kernels, on_device(): pl.pallas_call(kernel, out_shape=jax.ShapeDtypeStruct((NFREQ, 64, ROWS),...  58.1 us

profile of v6, /device:TPU:33, one launch (start us, length us, event | category | flops | bytes accessed | tf_op | source)
XLA Modules:
  0.0 58.9 jit_solution(5627807197747455884)
XLA Ops:
  0.0 58.1 %shard_map.82 = f32[16,64,128]{2,1,0:T(8,128)S(1)} custom-call(s32[8,128]{1,0:T(8,128)} %bitcast.4, s32[8,128]{1,0:T(8,128)} %bitcast.5, bf16[1024,2048]{1,0:T(8,128)(2,1)} %pw_hbm.1, bf16[2048,1024]{1,0:T(8,128)(2,1)} %basis_hbm.1, f32[64]{0:T(128)} %oe_hbm.1, f32[256]{0:T(256)} %ee_hbm.1, f32[16]{0:T(128)} %fg_hbm.1, s32[16]{0:T(128)} %fi_hbm.1), custom_call_target="tpu_custom_call" | custom-call | flops 9663676416 | bytes 9437184 | tf_op jit(solution)/shard_map/pallas_call | solution.py:503
  58.1 0.8 %copy.10 = f32[16,128,64]{1,2,0:T(8,128)} copy(f32[16,128,64]{1,2,0:T(8,128)S(1)} %bitcast.3) | data formatting | bytes 1048576
